TPU v7x, 32 devices: a whole 2x2x4 slice. The times are simulated.
32 devices in a mesh: groups: 2 (over y), fsdp: 4 (over x, core), tensor: 4 (over z).
Axes of the slice: x: 2, y: 2, z: 4, core: 2. Of those that a mesh axis runs over, the one named last changes fastest.
Arguments:
- tokens: bfloat16 [1024, 8192], P(('groups', 'fsdp')), parts along dimension 0, may hold values from -64 to 64
- gate_weight: bfloat16 [8192, 14336], P('fsdp', 'tensor'), may hold values from -0.0625 to 0.0625
- up_weight: bfloat16 [8192, 14336], P('fsdp', 'tensor'), may hold values from -0.0625 to 0.0625
- down_weight: bfloat16 [14336, 8192], P('tensor', 'fsdp'), may hold values from -0.046875 to 0.046875
- right_factor: bfloat16 [64, 128, 128], P('fsdp', 'tensor'), may hold values from -0.5 to 0.5
- left_factor: bfloat16 [128, 64, 64], P('fsdp', 'tensor'), may hold values from -0.75 to 0.75
Outputs:
- grad_right: float32 [128, 128, 128], P(('groups', 'fsdp'), 'tensor'), parts along dimension 0
- grad_left: float32 [256, 64, 64], P(('groups', 'fsdp'), 'tensor'), parts along dimension 0
There are 2 independent parts, one for each index of `groups`. A program takes and returns all parts, laid end to end along the dimension named above; an argument that names none is the same for every part. Nothing has to cross between parts.
All inputs are finite; a program needn't handle non-finite values.
Results may differ from a plain program's by a relative error of at most 0.0055.
Values may be sent and summed in bfloat16 or wider, within the bound.
A program may use at most 128 MiB of HBM per device.

v0:
```python
import math

import jax
import jax.numpy as jnp
from jax import lax
from jax.sharding import PartitionSpec as P


def body(tokens, gate_weight, up_weight, down_weight, right_factor, left_factor):
    fsdp_count = lax.axis_size("fsdp")
    tensor_count = lax.axis_size("tensor")
    tok_local = tokens.shape[0]
    group_rows = tok_local * fsdp_count
    share_rows = group_rows // tensor_count
    hid_local = gate_weight.shape[1]
    spread = lax.all_to_all(tokens, "fsdp", split_axis=1, concat_axis=0, tiled=True)
    student_in = lax.dynamic_slice_in_dim(
        spread, lax.axis_index("tensor") * share_rows, share_rows, 0
    )
    gate_part = jnp.dot(spread, gate_weight, preferred_element_type=jnp.float32)
    up_part = jnp.dot(spread, up_weight, preferred_element_type=jnp.float32)
    partial_value = jnp.concatenate([gate_part, up_part], axis=1)
    summed = lax.psum(partial_value.astype(jnp.bfloat16), "fsdp").astype(jnp.float32)
    hidden = (jax.nn.silu(summed[:, :hid_local]) * summed[:, hid_local:]).astype(jnp.bfloat16)
    target = lax.psum_scatter(
        jnp.dot(hidden, down_weight, preferred_element_type=jnp.float32).astype(jnp.bfloat16),
        "tensor",
        scatter_dimension=0,
        tiled=True,
    ).astype(jnp.float32)
    right_full, left_full = (
        lax.all_gather(right_factor, "tensor", axis=1, tiled=True),
        lax.all_gather(left_factor, "tensor", axis=1, tiled=True),
    )
    blocks_local = right_full.shape[0]
    block_size = right_full.shape[2]
    block_input = student_in.reshape(share_rows, blocks_local, block_size)
    mixed = jnp.einsum(
        "nij,ikj->nik", block_input, right_full, preferred_element_type=jnp.float32
    ).astype(jnp.bfloat16)
    routed = lax.all_to_all(mixed, "fsdp", split_axis=2, concat_axis=1, tiled=True)
    student = jnp.einsum("nij,jki->njk", routed, left_full, preferred_element_type=jnp.float32)
    inv_root = 1.0 / math.sqrt(group_rows)
    out_grad = (student - target.reshape(student.shape)) * inv_root
    grad_left = jnp.einsum("njk,nij->jki", out_grad, routed.astype(jnp.float32))
    mixed_grad = jnp.einsum("njk,jki->nij", out_grad, left_full.astype(jnp.float32)).astype(
        jnp.bfloat16
    )
    returned = lax.all_to_all(mixed_grad, "fsdp", split_axis=1, concat_axis=2, tiled=True)
    grad_right = jnp.einsum(
        "nik,nij->ikj", returned.astype(jnp.float32), block_input.astype(jnp.float32)
    )
    grad_right, grad_left = (
        lax.psum_scatter(grad_right, "tensor", scatter_dimension=1, tiled=True),
        lax.psum_scatter(grad_left, "tensor", scatter_dimension=1, tiled=True),
    )
    return (grad_right, grad_left)


def solution(mesh):
    return jax.shard_map(
        body,
        mesh=mesh,
        in_specs=(
            P(("groups", "fsdp"), None),
            P("fsdp", "tensor"),
            P("fsdp", "tensor"),
            P("tensor", "fsdp"),
            P("fsdp", "tensor", None),
            P("fsdp", "tensor", None),
        ),
        out_specs=(P(("groups", "fsdp"), "tensor", None), P(("groups", "fsdp"), "tensor", None)),
        check_vma=False,
    )
```

profile of v0, /device:TPU:2, one launch (start us, length us, event | category | flops | bytes accessed | tf_op | source)
XLA Modules:
  0.0 362.1 jit_solution(13968210217118573609)
XLA Ops:
  7.2 0.0 all-reduce.2.cloned.1.call-start
  7.2 4.1 %copy.27 = bf16[128,8192]{0,1:T(8,128)(2,1)} copy(bf16[128,8192]{1,0:T(8,128)(2,1)} %param.6) | data formatting | bytes 4194304 | tf_op args[0]
  11.3 27.3 %all_to_all.55 = bf16[128,4,2048]{0,2,1:T(8,128)(2,1)S(1)} all-to-all(bf16[128,4,2048]{0,2,1:T(8,128)(2,1)} %bitcast.39), channel_id=1, replica_groups=mesh['groups'=2,'fsdp'=4,'tensor'=4] {'fsdp'}, dimensions={1} | all-to-all | bytes 4194304 | tf_op jit(solution)/shard_map/all_to_all | solution.py:16
  38.6 2.6 copy.28
  41.3 0.0 copy-start
  41.3 13.7 %convolution_convert_fusion = bf16[512,3584]{1,0:T(8,128)(2,1)S(1)} fusion(bf16[512,2048]{1,0:T(8,128)(2,1)} %bitcast.45, bf16[2048,3584]{1,0:T(8,128)(2,1)} %param.8), kind=kOutput, calls=%fused_computation.3 | convolution fusion | flops 7518027776 | bytes 20447232 | tf_op jit(solution)/shard_map/dot_general | solution.py:21
  54.9 0.0 copy-done
  54.9 12.4 %convolution_convert_fusion.1 = bf16[512,3584]{1,0:T(8,128)(2,1)} fusion(bf16[512,2048]{1,0:T(8,128)(2,1)S(1)} %bitcast.47, bf16[2048,3584]{1,0:T(8,128)(2,1)} %param.7), kind=kOutput, calls=%fused_computation.4 | convolution fusion | flops 7518027776 | bytes 20447232 | tf_op jit(solution)/shard_map/dot_general | solution.py:20
  67.4 6.0 %pad_maximum_fusion = bf16[512,7168]{1,0:T(8,128)(2,1)} fusion(bf16[512,3584]{1,0:T(8,128)(2,1)S(1)} %convolution_convert_fusion, bf16[512,3584]{1,0:T(8,128)(2,1)} %convolution_convert_fusion.1), kind=kLoop, calls=%fused_computation.2 | loop fusion | flops 14680064 | bytes 14680064 | tf_op jit(solution)/shard_map/concatenate | solution.py:22
  73.3 0.0 all-reduce.2.cloned.1.call-update
  73.4 0.0 reduce-scatter.4.cloned.1.call-start
  73.4 138.1 %all-reduce.2.cloned.1.call-done = bf16[512,7168]{1,0:T(8,128)(2,1)} async-done(((bf16[512,7168]{1,0:T(8,128)(2,1)}), bf16[512,7168]{1,0:T(8,128)(2,1)}) %all-reduce.2.cloned.1.call-update) | async-done | bytes 7340048 | tf_op jit(solution)/shard_map/psum | solution.py:23
  211.5 10.2 %convert_element_type.29 = f32[512,7168]{1,0:T(8,128)} convert(bf16[512,7168]{1,0:T(8,128)(2,1)} %all-reduce.2.cloned.1.call-done) | non-fusion elementwise | flops 3670016 | bytes 22020096 | tf_op jit(solution)/shard_map/convert_element_type | solution.py:23
  221.7 0.0 copy-start.1
  221.7 16.5 %fusion.3 = bf16[512,2048]{1,0:T(8,128)(2,1)} fusion(bf16[3584,2048]{1,0:T(8,128)(2,1)} %param.9, f32[512,7168]{1,0:T(8,128)} %convert_element_type.29), kind=kOutput, calls=%fused_computation.6 | convolution fusion | flops 7528251392 | bytes 31457280 | tf_op jit(solution)/shard_map/dot_general | solution.py:26
  238.2 0.0 copy-start.2
  238.2 0.0 reduce-scatter.4.cloned.1.call-update
  238.2 0.0 copy-done.1
  238.3 21.3 %all_gather.6 = bf16[16,128,128]{2,1,0:T(8,128)(2,1)S(1)} all-gather(bf16[16,32,128]{2,1,0:T(8,128)(2,1)S(1)} %copy-done.1), channel_id=1, replica_groups=mesh['groups'=2,'fsdp'=4,'tensor'=4] {'tensor'}, dimensions={1}, use_global_device_ids=true | all-gather | bytes 655360 | tf_op jit(solution)/shard_map/all_gather | solution.py:32
  259.5 1.1 constant_dynamic-slice_fusion
  260.6 0.3 copy.29
  260.9 0.5 fusion.9
  261.4 1.2 copy.31
  262.6 5.9 %all-to-all-start.1 = ((bf16[128,16,128]{0,1,2:T(8,128)(2,1)}), bf16[128,16,128]{0,1,2:T(8,128)(2,1)S(1)}, u32[]{:S(2)}, u32[]{:S(2)}) async-start(bf16[128,16,128]{0,1,2:T(8,128)(2,1)} %copy.31), calls=%async_computation.1 | async-start | bytes 1048576 | tf_op jit(solution)/shard_map/all_to_all | solution.py:41
  268.5 0.0 reduce-scatter.8.cloned.1.call-start
  268.5 0.0 copy-done.2
  268.5 22.1 %all_gather.7 = bf16[32,64,64]{2,1,0:T(8,128)(2,1)S(1)} all-gather(bf16[32,16,64]{2,1,0:T(8,128)(2,1)S(1)} %copy-done.2), channel_id=1, replica_groups=mesh['groups'=2,'fsdp'=4,'tensor'=4] {'tensor'}, dimensions={1}, use_global_device_ids=true | all-gather | bytes 327680 | tf_op jit(solution)/shard_map/all_gather | solution.py:33
  290.6 0.0 all-to-all-done.1
  290.6 0.1 copy.33
  290.7 5.5 %reduce-scatter.4.cloned.1.call-done = bf16[128,2048]{1,0:T(8,128)(2,1)} async-done(((bf16[512,2048]{1,0:T(8,128)(2,1)}), bf16[128,2048]{1,0:T(8,128)(2,1)}) %reduce-scatter.4.cloned.1.call-update) | async-done | bytes 524304 | tf_op jit(solution)/shard_map/reduce_scatter | solution.py:25
  296.2 1.2 copy.34
  297.4 0.3 fusion.7
  297.7 1.4 fusion.12
  299.2 0.0 reduce-scatter.8.cloned.1.call-update
  299.2 0.0 reduce-scatter.6.cloned.1.call-start
  299.2 0.3 fusion.8
  299.6 0.3 copy.35
  299.9 10.3 %all_to_all.56 = bf16[128,64,32]{0,2,1:T(8,128)(2,1)S(1)} all-to-all(bf16[128,64,32]{0,2,1:T(8,128)(2,1)S(1)} %copy.35), channel_id=1, replica_groups=mesh['groups'=2,'fsdp'=4,'tensor'=4] {'fsdp'}, dimensions={1} | all-to-all | bytes 1048576 | tf_op jit(solution)/shard_map/all_to_all | solution.py:49
  310.3 1.5 fusion.11
  311.7 0.0 reduce-scatter.6.cloned.1.call-update
  311.7 15.2 %reduce-scatter.8.cloned.1.call-done = f32[32,16,64]{2,1,0:T(8,128)} async-done(((f32[32,64,64]{2,1,0:T(8,128)}), f32[32,16,64]{2,1,0:T(8,128)}) %reduce-scatter.8.cloned.1.call-update) | async-done | bytes 131088 | tf_op jit(solution)/shard_map/reduce_scatter | solution.py:55
  327.0 28.6 %reduce-scatter.6.cloned.1.call-done = f32[16,32,128]{2,1,0:T(8,128)} async-done(((f32[16,128,128]{2,1,0:T(8,128)}), f32[16,32,128]{2,1,0:T(8,128)}) %reduce-scatter.6.cloned.1.call-update) | async-done | bytes 262160 | tf_op jit(solution)/shard_map/reduce_scatter | solution.py:54
  (1 shorter events, 0.0 us)
Async XLA Ops:
  7.2 204.3 %all-reduce.2.cloned.1.call-start = ((), (), s32[]{:S(2)}) async-start(), calls=%async_computation.6 | async-start | bytes 14680064 | tf_op jit(solution)/shard_map/psum | solution.py:23
  41.3 13.7 %copy-start = (bf16[4,128,2048]{2,1,0:T(8,128)(2,1)S(1)}, bf16[4,128,2048]{2,1,0:T(8,128)(2,1)}, u32[]{:S(2)}) copy-start(bf16[4,128,2048]{2,1,0:T(8,128)(2,1)} %copy.28) | copy-start | bytes 6291460
  73.4 222.8 %reduce-scatter.4.cloned.1.call-start = ((), (), s32[]{:S(2)}) async-start(), calls=%async_computation.7 | async-start | bytes 2621440 | tf_op jit(solution)/shard_map/reduce_scatter | solution.py:25
  221.7 16.6 %copy-start.1 = (bf16[16,32,128]{2,1,0:T(8,128)(2,1)S(1)}, bf16[16,32,128]{2,1,0:T(8,128)(2,1)}, u32[]{:S(2)}) copy-start(bf16[16,32,128]{2,1,0:T(8,128)(2,1)} %param.10) | copy-start | bytes 393220
  238.2 30.3 %copy-start.2 = (bf16[32,16,64]{2,1,0:T(8,128)(2,1)S(1)}, bf16[32,16,64]{2,1,0:T(8,128)(2,1)}, u32[]{:S(2)}) copy-start(bf16[32,16,64]{2,1,0:T(8,128)(2,1)} %param.11) | copy-start | bytes 196612
  262.6 28.0 %all-to-all-start.1 = ((bf16[128,16,128]{0,1,2:T(8,128)(2,1)}), bf16[128,16,128]{0,1,2:T(8,128)(2,1)S(1)}, u32[]{:S(2)}, u32[]{:S(2)}) async-start(bf16[128,16,128]{0,1,2:T(8,128)(2,1)} %copy.31), calls=%async_computation.1 | async-start | bytes 1048576 | tf_op jit(solution)/shard_map/all_to_all | solution.py:41
  268.5 58.5 %reduce-scatter.8.cloned.1.call-start = ((), (), s32[]{:S(2)}) async-start(), calls=%async_computation.9 | async-start | bytes 1310720 | tf_op jit(solution)/shard_map/reduce_scatter | solution.py:55
  299.2 56.4 %reduce-scatter.6.cloned.1.call-start = ((), (), s32[]{:S(2)}) async-start(), calls=%async_computation.8 | async-start | bytes 1310720 | tf_op jit(solution)/shard_map/reduce_scatter | solution.py:54
Sparse Core Ops, SparseCore 0:
  73.5 137.9 all-reduce.1
  238.4 57.7 reduce-scatter.3
  299.3 27.6 reduce-scatter.7
  329.7 25.7 reduce-scatter.5
where the time goes:
time: 364 us; the launch traced here: 362 us
  waiting for transfers between devices  187 us (51%)
  blocking collectives  81 us (22%)
  matrix products  46.6 us (13%)
  other arithmetic  16.2 us (4%)
  between operations  13.8 us (4%)
  local copies, waits for them, and re-layouts  11 us (3%)
  starting transfers between devices  6.01 us (2%)
    psum x1, waiting for transfers between devices, body(): lax.psum(partial_value.astype(jnp.bfloat16), 'fsdp').astype(jnp.float32)  138 us
    reduce_scatter x1, waiting for transfers between devices, body(): lax.psum_scatter(grad_right, 'tensor', scatter_dimension=1, tiled=True)  28.6 us
    all_to_all x1, blocking collectives, body(): lax.all_to_all(tokens, 'fsdp', split_axis=1, concat_axis=0, tiled=True)  27.3 us
    all_gather x1, blocking collectives, body(): lax.all_gather(left_factor, 'tensor', axis=1, tiled=True)  22.1 us
    all_gather x1, blocking collectives, body(): lax.all_gather(right_factor, 'tensor', axis=1, tiled=True)  21.3 us
    dot_general x1, matrix products, body(): jnp.dot(hidden, down_weight, preferred_element_type=jnp.float32)  16.5 us
    reduce_scatter x1, waiting for transfers between devices, body(): lax.psum_scatter(grad_left, 'tensor', scatter_dimension=1, tiled=True)  15.2 us
    dot_general x1, matrix products, body(): up_part = jnp.dot(spread, up_weight, preferred_element_type=jnp.float32)  13.7 us
  transfers between devices with their start and end apart: 5, of which 4 were waited for; matrix products, arithmetic and copies ran while one was open for 1% of the time, Pallas kernels for 0%

commit v1 on v0

--- a/solution.py
+++ b/solution.py
@@ -1,12 +1,19 @@
+import functools
 import math
 
 import jax
 import jax.numpy as jnp
 from jax import lax
+from jax.experimental import pallas as pl
+from jax.experimental.pallas import tpu as pltpu
 from jax.sharding import PartitionSpec as P
 
-
-def body(tokens, gate_weight, up_weight, down_weight, right_factor, left_factor):
+MESH = pl.DeviceIdType.MESH
+CHUNK = 512
+PIECES = 4
+
+
+def plain_body(tokens, gate_weight, up_weight, down_weight, right_factor, left_factor):
     fsdp_count = lax.axis_size("fsdp")
     tensor_count = lax.axis_size("tensor")
     tok_local = tokens.shape[0]
@@ -57,6 +64,322 @@
     return (grad_right, grad_left)
 
 
+def teacher_kernel(
+    n, T, rows, width, cols,
+    tok, gw, uw, dw, spread, tgt,
+    wg, wu, wd, pbuf, recv_a, sbuf, recv_b, hid, acc, send_z, recv_z,
+    tok_send, tok_recv, w_sem, a_send, a_recv, b_send, b_recv,
+    hx_send, hx_recv, hp_send, hp_recv, r_send, r_recv, z_send, z_recv,
+):
+    f32, bf16 = jnp.float32, jnp.bfloat16
+    f = lax.axis_index("fsdp")
+    z = lax.axis_index("tensor")
+    x, c = f // 2, f % 2
+    partner = x * 2 + (1 - c)
+    across = (1 - x) * 2 + c
+    diag = (1 - x) * 2 + (1 - c)
+    q = c * 2 + x
+    q_across = c * 2 + (1 - x)
+    features = spread.shape[2]
+
+    def weights(t):
+        s = lax.rem(t, 2)
+        cc = pl.ds(pl.multiple_of(t * width, width), width)
+        return (
+            pltpu.make_async_copy(gw.at[:, cc], wg.at[s], w_sem.at[0, s]),
+            pltpu.make_async_copy(uw.at[:, cc], wu.at[s], w_sem.at[1, s]),
+        )
+
+    def down(t):
+        s = lax.rem(t, 2)
+        return pltpu.make_async_copy(
+            dw.at[pl.ds(pl.multiple_of(t * width, width), width), :], wd.at[s], w_sem.at[2, s]
+        )
+
+    for cp in weights(0):
+        cp.start()
+    down(0).start()
+
+    barrier = pltpu.get_barrier_semaphore()
+    for peer in (partner, across, diag):
+        pl.semaphore_signal(barrier, inc=1, device_id={"fsdp": peer}, device_id_type=MESH)
+
+    @pl.when(z > 0)
+    def _():
+        pl.semaphore_signal(barrier, inc=1, device_id={"tensor": z - 1}, device_id_type=MESH)
+
+    @pl.when(z < T - 1)
+    def _():
+        pl.semaphore_signal(barrier, inc=1, device_id={"tensor": z + 1}, device_id_type=MESH)
+
+    pl.semaphore_wait(barrier, 3 + (z + T - 1) // T + (2 * T - 2 - z) // T)
+
+    def tok_copy(i, peer):
+        cc = pl.ds(pl.multiple_of(peer * features, features), features)
+        return pltpu.make_async_remote_copy(
+            tok.at[:, cc], spread.at[q], tok_send.at[i], tok_recv.at[i],
+            device_id={"fsdp": peer}, device_id_type=MESH,
+        )
+
+    exchange = [tok_copy(0, across), tok_copy(1, diag), tok_copy(2, partner)]
+    for cp in exchange:
+        cp.start()
+    own = pltpu.make_async_copy(
+        tok.at[:, pl.ds(pl.multiple_of(f * features, features), features)],
+        spread.at[q], tok_send.at[3],
+    )
+    own.start()
+    acc[...] = jnp.zeros_like(acc)
+    own.wait()
+    for cp in exchange:
+        cp.wait()
+
+    def send_a(t):
+        return pltpu.make_async_remote_copy(
+            pbuf.at[t, 1 - c], recv_a.at[t], a_send.at[t], a_recv.at[t],
+            device_id={"fsdp": partner}, device_id_type=MESH)
+
+    def send_b(t):
+        return pltpu.make_async_remote_copy(
+            sbuf.at[t, 1 - x], recv_b.at[t], b_send.at[t], b_recv.at[t],
+            device_id={"fsdp": across}, device_id_type=MESH)
+
+    def send_hx(t):
+        return pltpu.make_async_remote_copy(
+            hid.at[t, q], hid.at[t, q], hx_send.at[t], hx_recv.at[t],
+            device_id={"fsdp": across}, device_id_type=MESH)
+
+    def send_hp(t):
+        return pltpu.make_async_remote_copy(
+            hid.at[t, q], hid.at[t, q], hp_send.at[t], hp_recv.at[t],
+            device_id={"fsdp": partner}, device_id_type=MESH)
+
+    def send_r(t):
+        return pltpu.make_async_remote_copy(
+            hid.at[t, q_across], hid.at[t, q_across], r_send.at[t], r_recv.at[t],
+            device_id={"fsdp": partner}, device_id_type=MESH)
+
+    def step(t, carry):
+        @pl.when(t < n)
+        def _():
+            @pl.when(t + 1 < n)
+            def _():
+                for cp in weights(t + 1):
+                    cp.start()
+
+            for cp in weights(t):
+                cp.wait()
+            s = lax.rem(t, 2)
+            toks = spread[...].reshape(4 * rows, features)
+            for k, w in ((0, wg), (1, wu)):
+                part = jnp.dot(toks, w[s], preferred_element_type=f32).astype(bf16)
+                for h in range(2):
+                    pbuf[t, h, k] = part[h * 2 * rows:(h + 1) * 2 * rows]
+            send_a(t).start()
+
+        @pl.when(t >= 3)
+        def _():
+            u = t - 3
+
+            @pl.when(u + 1 < n)
+            def _():
+                down(u + 1).start()
+
+            down(u).wait()
+            send_hp(u).wait_recv()
+            send_r(u).wait_recv()
+            s = lax.rem(u, 2)
+            h = hid[u].reshape(4 * rows, width)
+
+            @pl.loop(0, T)
+            def _(b):
+                cc = pl.ds(pl.multiple_of(b * cols, cols), cols)
+                acc[b] += jnp.dot(h, wd[s, :, cc], preferred_element_type=f32)
+
+        @pl.when(t < n)
+        def _():
+            send_a(t).wait_recv()
+            for k in range(2):
+                total = pbuf[t, c, k].astype(f32) + recv_a[t, k].astype(f32)
+                total = total.astype(bf16)
+                for h in range(2):
+                    sbuf[t, h, k] = total[h * rows:(h + 1) * rows]
+            send_b(t).start()
+
+        @pl.when((t >= 1) & (t < n + 1))
+        def _():
+            u = t - 1
+            send_b(u).wait_recv()
+            gate = sbuf[u, x, 0].astype(f32) + recv_b[u, 0].astype(f32)
+            up = sbuf[u, x, 1].astype(f32) + recv_b[u, 1].astype(f32)
+            hid[u, q] = (jax.nn.silu(gate) * up).astype(bf16)
+            send_hx(u).start()
+            send_hp(u).start()
+
+        @pl.when((t >= 2) & (t < n + 2))
+        def _():
+            u = t - 2
+            send_hx(u).wait_recv()
+            send_r(u).start()
+
+        return carry
+
+    lax.fori_loop(0, n + 3, step, 0)
+
+    piece = 4 * rows // PIECES
+
+    def send_right(d, s):
+        return pltpu.make_async_remote_copy(
+            send_z.at[0, d, s], recv_z.at[0, d, s], z_send.at[0, d, s], z_recv.at[0, d, s],
+            device_id={"tensor": z + 1}, device_id_type=MESH)
+
+    def send_left(d, s):
+        return pltpu.make_async_remote_copy(
+            send_z.at[1, d, s], recv_z.at[1, d, s], z_send.at[1, d, s], z_recv.at[1, d, s],
+            device_id={"tensor": z - 1}, device_id_type=MESH)
+
+    def hop(way, d, s, has_prev, sender):
+        rr = slice(s * piece, (s + 1) * piece)
+        mine = acc[d, rr].astype(bf16)
+        send_z[way, d, s] = mine
+
+        @pl.when(has_prev)
+        def _():
+            sender(d, s).wait_recv()
+            send_z[way, d, s] = (mine.astype(f32) + recv_z[way, d, s].astype(f32)).astype(bf16)
+
+        sender(d, s).start()
+
+    for j in range(T - 1):
+        for s in range(PIECES):
+            dr, dl = T - 1 - j, j
+
+            @pl.when(z < dr)
+            def _():
+                hop(0, dr, s, z > 0, send_right)
+
+            @pl.when(z > dl)
+            def _():
+                hop(1, dl, s, z < T - 1, send_left)
+
+    for s in range(PIECES):
+        rr = slice(s * piece, (s + 1) * piece)
+        tgt[rr] = acc[z, rr].astype(bf16).astype(f32)
+
+        @pl.when(z > 0)
+        def _():
+            send_right(z, s).wait_recv()
+            tgt[rr] += recv_z[0, z, s].astype(f32)
+
+        @pl.when(z < T - 1)
+        def _():
+            send_left(z, s).wait_recv()
+            tgt[rr] += recv_z[1, z, s].astype(f32)
+
+    for j in range(T - 1):
+        for s in range(PIECES):
+            dr, dl = T - 1 - j, j
+
+            @pl.when(z < dr)
+            def _():
+                send_right(dr, s).wait_send()
+
+            @pl.when(z > dl)
+            def _():
+                send_left(dl, s).wait_send()
+
+    def drain(t, carry):
+        for sender in (send_a, send_b, send_hx, send_hp, send_r):
+            sender(t).wait_send()
+        return carry
+
+    lax.fori_loop(0, n, drain, 0)
+
+
+def teacher(tokens, gate_weight, up_weight, down_weight, T):
+    rows = tokens.shape[0]
+    features, hidden = gate_weight.shape
+    width = CHUNK
+    n = hidden // width
+    cols = down_weight.shape[1] // T
+    bf16, f32 = jnp.bfloat16, jnp.float32
+    dma = pltpu.SemaphoreType.DMA
+    anyspace = pl.BlockSpec(memory_space=pl.ANY)
+    vmem = pl.BlockSpec(memory_space=pltpu.VMEM)
+    return pl.pallas_call(
+        functools.partial(teacher_kernel, n, T, rows, width, cols),
+        out_shape=(
+            jax.ShapeDtypeStruct((4, rows, features), bf16),
+            jax.ShapeDtypeStruct((4 * rows, cols), f32),
+        ),
+        in_specs=[anyspace] * 4,
+        out_specs=(vmem, vmem),
+        scratch_shapes=[
+            pltpu.VMEM((2, features, width), bf16),
+            pltpu.VMEM((2, features, width), bf16),
+            pltpu.VMEM((2, width, T * cols), bf16),
+            pltpu.VMEM((n, 2, 2, 2 * rows, width), bf16),
+            pltpu.VMEM((n, 2, 2 * rows, width), bf16),
+            pltpu.VMEM((n, 2, 2, rows, width), bf16),
+            pltpu.VMEM((n, 2, rows, width), bf16),
+            pltpu.VMEM((n, 4, rows, width), bf16),
+            pltpu.VMEM((T, 4 * rows, cols), f32),
+            pltpu.VMEM((2, T, PIECES, 4 * rows // PIECES, cols), bf16),
+            pltpu.VMEM((2, T, PIECES, 4 * rows // PIECES, cols), bf16),
+            dma((4,)), dma((3,)), dma((3, 2)),
+            dma((n,)), dma((n,)), dma((n,)), dma((n,)),
+            dma((n,)), dma((n,)), dma((n,)), dma((n,)), dma((n,)), dma((n,)),
+            dma((2, T, PIECES)), dma((2, T, PIECES)),
+        ],
+        compiler_params=pltpu.CompilerParams(
+            collective_id=0, has_side_effects=True, vmem_limit_bytes=62 * 1024 * 1024
+        ),
+        name="teacher",
+    )(tokens, gate_weight, up_weight, down_weight)
+
+
+def fused_body(tokens, gate_weight, up_weight, down_weight, right_factor, left_factor):
+    T = lax.axis_size("tensor")
+    rows = tokens.shape[0] * lax.axis_size("fsdp")
+    right = lax.all_to_all(right_factor, "tensor", split_axis=1, concat_axis=1, tiled=True)
+    left = lax.all_to_all(left_factor, "tensor", split_axis=0, concat_axis=1, tiled=True)
+    spread, target = teacher(tokens, gate_weight, up_weight, down_weight, T)
+    blocks, size = right.shape[0], right.shape[2]
+    block_input = spread.reshape(rows, blocks, size)
+    mixed = jnp.einsum(
+        "nij,ikj->nik", block_input, right, preferred_element_type=jnp.float32
+    ).astype(jnp.bfloat16)
+    routed = lax.all_to_all(mixed, "fsdp", split_axis=2, concat_axis=1, tiled=True)
+    student = jnp.einsum("nij,jki->njk", routed, left, preferred_element_type=jnp.float32)
+    out_grad = (student - target.reshape(student.shape)) * (1.0 / math.sqrt(rows))
+    grad_left = jnp.einsum("njk,nij->jki", out_grad, routed.astype(jnp.float32))
+    mixed_grad = jnp.einsum("njk,jki->nij", out_grad, left.astype(jnp.float32)).astype(
+        jnp.bfloat16
+    )
+    returned = lax.all_to_all(mixed_grad, "fsdp", split_axis=1, concat_axis=2, tiled=True)
+    grad_right = jnp.einsum(
+        "nik,nij->ikj", returned.astype(jnp.float32), block_input.astype(jnp.float32)
+    )
+    grad_right = lax.all_to_all(grad_right, "tensor", split_axis=1, concat_axis=1, tiled=True)
+    grad_left = lax.all_to_all(grad_left, "tensor", split_axis=1, concat_axis=0, tiled=True)
+    return (grad_right, grad_left)
+
+
+def body(tokens, gate_weight, up_weight, down_weight, right_factor, left_factor):
+    F, T = lax.axis_size("fsdp"), lax.axis_size("tensor")
+    fits = (
+        F == 4
+        and T == 4
+        and gate_weight.shape[1] % CHUNK == 0
+        and left_factor.shape[0] % T == 0
+        and right_factor.shape[1] % T == 0
+        and gate_weight.shape[0] <= 2048
+        and tokens.shape[0] == 128
+    )
+    run = fused_body if fits else plain_body
+    return run(tokens, gate_weight, up_weight, down_weight, right_factor, left_factor)
+
+
 def solution(mesh):
     return jax.shard_map(
         body,

time: 364 us -> 215 us (0.59)
  waiting for transfers between devices: 187 us -> 25.6 us
  Pallas kernels: 0 us -> 139 us
  blocking collectives: 81 us -> 0 us
  matrix products: 46.6 us -> 3.67 us
  starting transfers between devices: 6.01 us -> 30 us
  other arithmetic: 16.2 us -> 0.98 us
  between operations: 13.8 us -> 0.77 us
    pallas_call x0 -> x1, Pallas kernels: none -> 139 us  [teacher(): pl.pallas_call(functools.partial(teacher_kernel, n, T, rows, width, cols)...]
    psum x1 -> x0, waiting for transfers between devices: 138 us -> none  [body(): lax.psum(partial_value.astype(jnp.bfloat16), 'fsdp').astype(jnp.float32)]
    reduce_scatter x3 -> x0, waiting for transfers between devices: 49.3 us -> none  [the longest x1 28.6 us: body(): lax.psum_scatter(grad_right, 'tensor', scatter_dimension=1, tiled=True)]
    all_gather x2 -> x0, blocking collectives: 43.4 us -> none  [the longest x1 22.1 us: body(): lax.all_gather(left_factor, 'tensor', axis=1, tiled=True)]
    dot_general x8 -> x5, matrix products: 46.6 us -> 3.67 us  [the longest x1 1.79 us: fused_body(): jnp.einsum('nik,nij->ikj', returned.astype(jnp.float32), block_input.asty...]
    all_to_all x2 -> x0, blocking collectives: 37.6 us -> none  [the longest x1 27.3 us: body(): lax.all_to_all(tokens, 'fsdp', split_axis=1, concat_axis=0, tiled=True)]
    all_to_all x1 -> x6, waiting for transfers between devices: 0.01 us -> 25.6 us  [the longest x1 6.67 us: fused_body(): lax.all_to_all(mixed, 'fsdp', split_axis=2, concat_axis=1, tiled=True)]
    all_to_all x1 -> x6, starting transfers between devices: 5.89 us -> 30 us  [the longest x1 7.04 us: fused_body(): lax.all_to_all(left_factor, 'tensor', split_axis=0, concat_axis=1, tiled=...]
  transfers between devices with their start and end apart: 5 -> 6, of which waited for: 4 -> 5; matrix products, arithmetic and copies ran while one was open for 1% -> 6% of each run, Pallas kernels for 0% -> 66%
where the time goes in v1:
time: 215 us; the launch traced here: 212 us
  Pallas kernels  139 us (65%)
  starting transfers between devices  30 us (14%)
  waiting for transfers between devices  25.6 us (12%)
  local copies, waits for them, and re-layouts  11.6 us (5%)
  matrix products  3.67 us (2%)
    pallas_call x1, Pallas kernels, teacher(): pl.pallas_call(functools.partial(teacher_kernel, n, T, rows, width, cols)...  139 us
    all_to_all x1, starting transfers between devices, fused_body(): lax.all_to_all(left_factor, 'tensor', split_axis=0, concat_axis=1, tiled=...  7.04 us
    unnamed x15, local copies, waits for them, and re-layouts  6.78 us
    all_to_all x1, waiting for transfers between devices, fused_body(): lax.all_to_all(mixed, 'fsdp', split_axis=2, concat_axis=1, tiled=True)  6.67 us
    all_to_all x1, waiting for transfers between devices, fused_body(): lax.all_to_all(mixed_grad, 'fsdp', split_axis=1, concat_axis=2, tiled=True)  6.01 us
    all_to_all x1, starting transfers between devices, fused_body(): lax.all_to_all(mixed_grad, 'fsdp', split_axis=1, concat_axis=2, tiled=True)  5.76 us
    all_to_all x1, waiting for transfers between devices, fused_body(): lax.all_to_all(grad_right, 'tensor', split_axis=1, concat_axis=1, tiled=T...  5.7 us
    all_to_all x1, starting transfers between devices, fused_body(): lax.all_to_all(mixed, 'fsdp', split_axis=2, concat_axis=1, tiled=True)  5.6 us
  transfers between devices with their start and end apart: 6, of which 5 were waited for; matrix products, arithmetic and copies ran while one was open for 6% of the time, Pallas kernels for 66%

profile of v1, /device:TPU:2, one launch (start us, length us, event | category | flops | bytes accessed | tf_op | source)
XLA Modules:
  0.0 211.6 jit_solution(17189637899368914465)
XLA Ops:
  0.6 1.6 copy.24
  2.2 4.9 %all-to-all-start = ((bf16[16,32,128]{2,0,1:T(8,128)(2,1)}), bf16[16,32,128]{2,0,1:T(8,128)(2,1)S(1)}, u32[]{:S(2)}, u32[]{:S(2)}) async-start(bf16[16,32,128]{2,0,1:T(8,128)(2,1)} %copy.24), calls=%async_computation | async-start | bytes 262144 | tf_op jit(solution)/shard_map/all_to_all | solution.py:344
  7.1 138.9 %teacher.1 = (bf16[4,128,2048]{2,1,0:T(8,128)(2,1)}, f32[512,512]{1,0:T(8,128)}) custom-call(bf16[128,8192]{1,0:T(8,128)(2,1)} %tok.1, bf16[2048,3584]{1,0:T(8,128)(2,1)} %gw.1, bf16[2048,3584]{1,0:T(8,128)(2,1)} %uw.1, bf16[3584,2048]{1,0:T(8,128)(2,1)} %dw.1), custom_call_target="tpu_custom_call" | custom-call | tf_op jit(solution)/shard_map/teacher/pallas_call | solution.py:309
  146.1 0.0 copy-start.3
  146.1 2.2 %copy.40 = bf16[64,8,16,128]{3,2,1,0:T(8,128)(2,1)S(1)} copy(bf16[64,8,16,128]{3,1,2,0:T(8,128)(2,1)} %bitcast.47) | data formatting | bytes 4194304
  148.3 0.0 copy-done.3
  148.3 0.0 copy-start
  148.3 1.0 reshape.12
  149.3 0.0 all-to-all-done
  149.3 7.0 %all-to-all-start.2 = ((bf16[4,2,4096]{2,1,0:T(2,128)(2,1)}), bf16[4,2,4096]{2,1,0:T(2,128)(2,1)S(1)}, u32[]{:S(2)}, u32[]{:S(2)}) async-start(bf16[4,2,4096]{2,1,0:T(2,128)(2,1)} %reshape.12), calls=%async_computation.2 | async-start | bytes 131072 | tf_op jit(solution)/shard_map/all_to_all | solution.py:345
  156.3 0.0 copy-start.2
  156.3 1.0 fusion.9
  157.3 1.1 copy.27
  158.4 0.0 copy-done
  158.4 3.6 %all-to-all-done.2 = bf16[4,2,4096]{2,1,0:T(2,128)(2,1)S(1)} async-done(((bf16[4,2,4096]{2,1,0:T(2,128)(2,1)}), bf16[4,2,4096]{2,1,0:T(2,128)(2,1)S(1)}, u32[]{:S(2)}, u32[]{:S(2)}) %all-to-all-start.2) | async-done | bytes 65568 | tf_op jit(solution)/shard_map/all_to_all | solution.py:345
  162.1 5.6 %all-to-all-start.1 = ((bf16[512,16,32]{0,1,2:T(8,128)(2,1)}), bf16[512,16,32]{0,1,2:T(8,128)(2,1)S(1)}, u32[]{:S(2)}, u32[]{:S(2)}) async-start(bf16[512,16,32]{0,1,2:T(8,128)(2,1)} %copy.27), calls=%async_computation.1 | async-start | bytes 1048576 | tf_op jit(solution)/shard_map/all_to_all | solution.py:352
  167.7 0.0 copy-done.2
  167.7 0.3 copy.30
  168.0 0.1 reshape.13
  168.2 6.7 %all-to-all-done.1 = bf16[512,16,32]{0,1,2:T(8,128)(2,1)S(1)} async-done(((bf16[512,16,32]{0,1,2:T(8,128)(2,1)}), bf16[512,16,32]{0,1,2:T(8,128)(2,1)S(1)}, u32[]{:S(2)}, u32[]{:S(2)}) %all-to-all-start.1) | async-done | bytes 524320 | tf_op jit(solution)/shard_map/all_to_all | solution.py:352
  174.9 0.3 fusion.5
  175.2 0.3 fusion.12
  175.5 0.0 copy-start.1
  175.5 1.1 copy.32
  176.6 5.8 %all-to-all-start.3 = ((bf16[512,64,8]{0,2,1:T(8,128)(2,1)}), bf16[512,64,8]{0,2,1:T(8,128)(2,1)}, u32[]{:S(2)}, u32[]{:S(2)}) async-start(bf16[512,64,8]{0,2,1:T(8,128)(2,1)} %copy.32), calls=%async_computation.3 | async-start | bytes 1048576 | tf_op jit(solution)/shard_map/all_to_all | solution.py:359
  182.4 0.3 fusion.16
  182.7 0.2 copy.56
  182.8 0.8 reshape.14
  183.7 6.0 %all-to-all-done.3 = bf16[512,64,8]{0,2,1:T(8,128)(2,1)} async-done(((bf16[512,64,8]{0,2,1:T(8,128)(2,1)}), bf16[512,64,8]{0,2,1:T(8,128)(2,1)}, u32[]{:S(2)}, u32[]{:S(2)}) %all-to-all-start.3) | async-done | bytes 524320 | tf_op jit(solution)/shard_map/all_to_all | solution.py:359
  189.7 3.3 %all-to-all-start.5 = ((f32[4,1,8192]{2,1,0:T(1,128)}), f32[4,1,8192]{2,1,0:T(1,128)S(1)}, u32[]{:S(2)}, u32[]{:S(2)}) async-start(f32[4,1,8192]{2,1,0:T(1,128)} %reshape.14), calls=%async_computation.5 | async-start | bytes 262144 | tf_op jit(solution)/shard_map/all_to_all | solution.py:364
  193.0 0.0 copy-done.1
  193.0 1.8 fusion
  194.8 0.9 copy.35
  195.7 3.6 %all-to-all-done.5 = f32[4,1,8192]{2,1,0:T(1,128)S(1)} async-done(((f32[4,1,8192]{2,1,0:T(1,128)}), f32[4,1,8192]{2,1,0:T(1,128)S(1)}, u32[]{:S(2)}, u32[]{:S(2)}) %all-to-all-start.5) | async-done | bytes 131104 | tf_op jit(solution)/shard_map/all_to_all | solution.py:364
  199.2 3.4 %all-to-all-start.4 = ((f32[16,32,128]{2,0,1:T(8,128)}), f32[16,32,128]{2,0,1:T(8,128)S(1)}, u32[]{:S(2)}, u32[]{:S(2)}) async-start(f32[16,32,128]{2,0,1:T(8,128)} %copy.35), calls=%async_computation.4 | async-start | bytes 524288 | tf_op jit(solution)/shard_map/all_to_all | solution.py:363
  202.7 0.5 broadcast
  203.2 1.0 reduce
  204.2 0.2 reshape.15
  204.3 0.8 copy.37
  205.1 5.7 %all-to-all-done.4 = f32[16,32,128]{2,0,1:T(8,128)S(1)} async-done(((f32[16,32,128]{2,0,1:T(8,128)}), f32[16,32,128]{2,0,1:T(8,128)S(1)}, u32[]{:S(2)}, u32[]{:S(2)}) %all-to-all-start.4) | async-done | bytes 262176 | tf_op jit(solution)/shard_map/all_to_all | solution.py:363
  210.8 0.8 copy.38
  (2 shorter events, 0.0 us)
Async XLA Ops:
  2.2 147.1 %all-to-all-start = ((bf16[16,32,128]{2,0,1:T(8,128)(2,1)}), bf16[16,32,128]{2,0,1:T(8,128)(2,1)S(1)}, u32[]{:S(2)}, u32[]{:S(2)}) async-start(bf16[16,32,128]{2,0,1:T(8,128)(2,1)} %copy.24), calls=%async_computation | async-start | bytes 262144 | tf_op jit(solution)/shard_map/all_to_all | solution.py:344
  146.1 2.3 %copy-start.3 = (bf16[32,16,64]{2,1,0:T(8,128)(2,1)S(1)}, bf16[32,16,64]{2,1,0:T(8,128)(2,1)}, u32[]{:S(2)}) copy-start(bf16[32,16,64]{2,1,0:T(8,128)(2,1)} %param.11) | copy-start | bytes 196612
  148.3 10.1 %copy-start = (bf16[64,8,16,128]{3,2,1,0:T(8,128)(2,1)}, bf16[64,8,16,128]{3,2,1,0:T(8,128)(2,1)S(1)}, u32[]{:S(2)}) copy-start(bf16[64,8,16,128]{3,2,1,0:T(8,128)(2,1)S(1)} %copy.40) | copy-start | bytes 6291460
  149.3 12.8 %all-to-all-start.2 = ((bf16[4,2,4096]{2,1,0:T(2,128)(2,1)}), bf16[4,2,4096]{2,1,0:T(2,128)(2,1)S(1)}, u32[]{:S(2)}, u32[]{:S(2)}) async-start(bf16[4,2,4096]{2,1,0:T(2,128)(2,1)} %reshape.12), calls=%async_computation.2 | async-start | bytes 131072 | tf_op jit(solution)/shard_map/all_to_all | solution.py:345
  156.3 11.3 %copy-start.2 = (f32[512,512]{1,0:T(8,128)S(1)}, f32[512,512]{1,0:T(8,128)}, u32[]{:S(2)}) copy-start(f32[512,512]{1,0:T(8,128)} %get-tuple-element.5) | copy-start | bytes 3145732
  162.1 12.8 %all-to-all-start.1 = ((bf16[512,16,32]{0,1,2:T(8,128)(2,1)}), bf16[512,16,32]{0,1,2:T(8,128)(2,1)S(1)}, u32[]{:S(2)}, u32[]{:S(2)}) async-start(bf16[512,16,32]{0,1,2:T(8,128)(2,1)} %copy.27), calls=%async_computation.1 | async-start | bytes 1048576 | tf_op jit(solution)/shard_map/all_to_all | solution.py:352
  175.5 17.5 %copy-start.1 = (bf16[64,8,16,128]{3,2,1,0:T(8,128)(2,1)S(1)}, bf16[64,8,16,128]{3,2,1,0:T(8,128)(2,1)}, u32[]{:S(2)}) copy-start(bf16[64,8,16,128]{3,2,1,0:T(8,128)(2,1)} %copy-done) | copy-start | bytes 6291460
  176.6 13.0 %all-to-all-start.3 = ((bf16[512,64,8]{0,2,1:T(8,128)(2,1)}), bf16[512,64,8]{0,2,1:T(8,128)(2,1)}, u32[]{:S(2)}, u32[]{:S(2)}) async-start(bf16[512,64,8]{0,2,1:T(8,128)(2,1)} %copy.32), calls=%async_computation.3 | async-start | bytes 1048576 | tf_op jit(solution)/shard_map/all_to_all | solution.py:359
  189.7 9.6 %all-to-all-start.5 = ((f32[4,1,8192]{2,1,0:T(1,128)}), f32[4,1,8192]{2,1,0:T(1,128)S(1)}, u32[]{:S(2)}, u32[]{:S(2)}) async-start(f32[4,1,8192]{2,1,0:T(1,128)} %reshape.14), calls=%async_computation.5 | async-start | bytes 262144 | tf_op jit(solution)/shard_map/all_to_all | solution.py:364
  199.2 11.6 %all-to-all-start.4 = ((f32[16,32,128]{2,0,1:T(8,128)}), f32[16,32,128]{2,0,1:T(8,128)S(1)}, u32[]{:S(2)}, u32[]{:S(2)}) async-start(f32[16,32,128]{2,0,1:T(8,128)} %copy.35), calls=%async_computation.4 | async-start | bytes 524288 | tf_op jit(solution)/shard_map/all_to_all | solution.py:363

commit v2 on v1

--- a/solution.py
+++ b/solution.py
@@ -64,12 +64,15 @@
     return (grad_right, grad_left)
 
 
-def teacher_kernel(
+def layer_kernel(
     n, T, rows, width, cols,
-    tok, gw, uw, dw, spread, tgt,
+    tok, gw, uw, dw, right, left, gr_out, gl_out,
     wg, wu, wd, pbuf, recv_a, sbuf, recv_b, hid, acc, send_z, recv_z,
+    spread, tgt, rki, lji, rbig, lbig, mix_s, routed, student, mg_s, mg_r, gr_s, gl_s,
     tok_send, tok_recv, w_sem, a_send, a_recv, b_send, b_recv,
     hx_send, hx_recv, hp_send, hp_recv, r_send, r_recv, z_send, z_recv,
+    rf_send, rf_recv, lf_send, lf_recv, mix_send, mix_recv, mg_send, mg_recv,
+    gr_send, gr_recv, gl_send, gl_recv,
 ):
     f32, bf16 = jnp.float32, jnp.bfloat16
     f = lax.axis_index("fsdp")
@@ -104,15 +107,10 @@
     for peer in (partner, across, diag):
         pl.semaphore_signal(barrier, inc=1, device_id={"fsdp": peer}, device_id_type=MESH)
 
-    @pl.when(z > 0)
-    def _():
-        pl.semaphore_signal(barrier, inc=1, device_id={"tensor": z - 1}, device_id_type=MESH)
-
-    @pl.when(z < T - 1)
-    def _():
-        pl.semaphore_signal(barrier, inc=1, device_id={"tensor": z + 1}, device_id_type=MESH)
-
-    pl.semaphore_wait(barrier, 3 + (z + T - 1) // T + (2 * T - 2 - z) // T)
+    for d in range(1, T):
+        pl.semaphore_signal(
+            barrier, inc=1, device_id={"tensor": lax.rem(z + d, T)}, device_id_type=MESH)
+    pl.semaphore_wait(barrier, 3 + T - 1)
 
     def tok_copy(i, peer):
         cc = pl.ds(pl.multiple_of(peer * features, features), features)
@@ -130,9 +128,67 @@
     )
     own.start()
     acc[...] = jnp.zeros_like(acc)
+
+    N = 4 * rows
+    na, ni, nj = rki.shape[1:]
+    nk, nf = lji.shape[2] * T, na * ni
+    nb = lji.shape[3]
+
+    def right_copy(d):
+        peer = lax.rem(z + d, T)
+        return pltpu.make_async_remote_copy(
+            right.at[pl.ds(peer * na, na)], rki.at[z], rf_send.at[d], rf_recv.at[d],
+            device_id={"tensor": peer}, device_id_type=MESH)
+
+    def left_copy(d):
+        peer = lax.rem(z + d, T)
+        return pltpu.make_async_remote_copy(
+            left.at[pl.ds(peer * na, na)], lji.at[:, z], lf_send.at[d], lf_recv.at[d],
+            device_id={"tensor": peer}, device_id_type=MESH)
+
+    factors = [right_copy(d) for d in range(1, T)] + [left_copy(d) for d in range(1, T)]
+    for cp in factors:
+        cp.start()
+    own_right = pltpu.make_async_copy(right.at[pl.ds(z * na, na)], rki.at[z], rf_send.at[0])
+    own_left = pltpu.make_async_copy(left.at[pl.ds(z * na, na)], lji.at[:, z], lf_send.at[0])
+    own_right.start()
+    own_left.start()
+    own_right.wait()
+    own_left.wait()
+    for cp in factors:
+        cp.wait()
+
+    iota = functools.partial(lax.broadcasted_iota, jnp.int32)
+    packed = rki[...].reshape(T * nf, nj)
+    lane_block = lax.rem(iota((T * nf, nj), 0), ni)
+    for i in range(ni):
+        rbig[:, i * nj:(i + 1) * nj] = jnp.where(lane_block == i, packed, jnp.zeros_like(packed))
+    col = iota((nb, 4 * nf), 1)
+    pick = iota((nb, 4 * nf), 0) == (col // nf) * ni + lax.rem(col, ni)
+    wide = jnp.dot(
+        lji[...].reshape(na * nk, nb), pick.astype(f32).astype(bf16), preferred_element_type=f32)
+    same = iota((na * nk, 4 * nf), 0) // nk == lax.rem(iota((na * nk, 4 * nf), 1), nf) // ni
+    lbig[...] = jnp.where(same, wide, 0.0).astype(bf16)
+
     own.wait()
     for cp in exchange:
         cp.wait()
+
+    peers = (across, diag, partner)
+
+    def mix_copy(i):
+        return pltpu.make_async_remote_copy(
+            mix_s.at[peers[i]], routed.at[f], mix_send.at[i], mix_recv.at[i],
+            device_id={"fsdp": peers[i]}, device_id_type=MESH)
+
+    mixed = lax.dot_general(
+        spread[...].reshape(N, features), rbig[...], (((1,), (1,)), ((), ())),
+        preferred_element_type=f32).astype(bf16)
+    for g in range(4):
+        mix_s[g] = mixed[:, g * nf:(g + 1) * nf]
+    for i in range(3):
+        mix_copy(i).start()
+    routed[f] = mix_s[f]
 
     def send_a(t):
         return pltpu.make_async_remote_copy(
@@ -216,6 +272,17 @@
             send_hx(u).start()
             send_hp(u).start()
 
+        @pl.when(t == 2)
+        def _():
+            for i in range(3):
+                mix_copy(i).wait_recv()
+            total = jnp.zeros((N, na * nk), f32)
+            for g in range(4):
+                total += lax.dot_general(
+                    routed[g], lbig[:, g * nf:(g + 1) * nf], (((1,), (1,)), ((), ())),
+                    preferred_element_type=f32)
+            student[...] = total
+
         @pl.when((t >= 2) & (t < n + 2))
         def _():
             u = t - 2
@@ -276,6 +343,84 @@
             send_left(z, s).wait_recv()
             tgt[rr] += recv_z[1, z, s].astype(f32)
 
+    def mg_copy(i):
+        return pltpu.make_async_remote_copy(
+            mg_s.at[peers[i]], mg_r.at[f], mg_send.at[i], mg_recv.at[i],
+            device_id={"fsdp": peers[i]}, device_id_type=MESH)
+
+    def gl_copy(d):
+        peer = lax.rem(z + d, T)
+        return pltpu.make_async_remote_copy(
+            gl_s.at[:, peer], gl_out.at[pl.ds(z * na, na)], gl_send.at[d], gl_recv.at[d],
+            device_id={"tensor": peer}, device_id_type=MESH)
+
+    def gr_copy(g):
+        return pltpu.make_async_remote_copy(
+            gr_s.at[g], gr_out.at[z], gr_send.at[g], gr_recv.at[z],
+            device_id={"tensor": g}, device_id_type=MESH)
+
+    out_grad = (student[...] - tgt[...]) * (1.0 / math.sqrt(N))
+    narrow = out_grad.astype(bf16)
+    mixed_grad = jnp.dot(narrow, lbig[...], preferred_element_type=f32).astype(bf16)
+    for g in range(4):
+        mg_s[g] = mixed_grad[:, g * nf:(g + 1) * nf]
+    for i in range(3):
+        mg_copy(i).start()
+    mg_r[f] = mg_s[f]
+
+    turned = out_grad.T.astype(bf16)
+    keep = iota((na * nk, nf), 0) // nk == iota((na * nk, nf), 1) // ni
+    total = jnp.zeros((na * nk, nb), f32)
+    for g in range(4):
+        part = jnp.dot(turned, routed[g], preferred_element_type=f32)
+        fold = iota((nf, nb), 1) == g * ni + lax.rem(iota((nf, nb), 0), ni)
+        total += jnp.dot(
+            jnp.where(keep, part, 0.0), fold.astype(f32),
+            precision=lax.Precision.HIGHEST, preferred_element_type=f32)
+    gl_s[...] = total.reshape(na, T, nk // T, nb)
+    for d in range(1, T):
+        gl_copy(d).start()
+    gl_out[pl.ds(z * na, na)] = gl_s[:, z]
+
+    row_block = lax.rem(iota((nf, nj), 0), ni)
+
+    def grad_right(g):
+        flipped = mg_r[g].astype(f32).T.astype(bf16)
+        total = jnp.zeros((nf, nj), f32)
+        for i in range(0, ni, 2):
+            rhs = spread[:, :, i * nj:(i + 2) * nj].reshape(N, 2 * nj)
+            part = jnp.dot(flipped, rhs, preferred_element_type=f32)
+            for k in range(2):
+                total += jnp.where(row_block == i + k, part[:, k * nj:(k + 1) * nj], 0.0)
+        gr_s[g] = total.reshape(na, ni, nj)
+
+        @pl.when(g != z)
+        def _():
+            gr_copy(g).start()
+
+        @pl.when(g == z)
+        def _():
+            gr_out[z] = gr_s[g]
+
+    grad_right(f)
+    for i in (2, 0, 1):
+        mg_copy(i).wait_recv()
+        grad_right(peers[i])
+
+    for d in range(1, T):
+        gl_copy(d).wait()
+    for g in range(T):
+        @pl.when(z != g)
+        def _():
+            gr_copy(g).wait_send()
+            pltpu.make_async_remote_copy(
+                gr_s.at[g], gr_out.at[g], gr_send.at[g], gr_recv.at[g],
+                device_id={"tensor": g}, device_id_type=MESH).wait_recv()
+
+    for i in range(3):
+        mix_copy(i).wait_send()
+        mg_copy(i).wait_send()
+
     for j in range(T - 1):
         for s in range(PIECES):
             dr, dl = T - 1 - j, j
@@ -296,7 +441,9 @@
     lax.fori_loop(0, n, drain, 0)
 
 
-def teacher(tokens, gate_weight, up_weight, down_weight, T):
+def fused_body(tokens, gate_weight, up_weight, down_weight, right_factor, left_factor):
+    T = lax.axis_size("tensor")
+    right = jnp.transpose(right_factor, (1, 0, 2))
     rows = tokens.shape[0]
     features, hidden = gate_weight.shape
     width = CHUNK
@@ -306,13 +453,16 @@
     dma = pltpu.SemaphoreType.DMA
     anyspace = pl.BlockSpec(memory_space=pl.ANY)
     vmem = pl.BlockSpec(memory_space=pltpu.VMEM)
-    return pl.pallas_call(
-        functools.partial(teacher_kernel, n, T, rows, width, cols),
+    ni, nkr, nj = right_factor.shape
+    na, nkl, nb = left_factor.shape[0] // T, left_factor.shape[1], left_factor.shape[2]
+    nf, nk = na * ni, nkl * T
+    grad_right, grad_left = pl.pallas_call(
+        functools.partial(layer_kernel, n, T, rows, width, cols),
         out_shape=(
-            jax.ShapeDtypeStruct((4, rows, features), bf16),
-            jax.ShapeDtypeStruct((4 * rows, cols), f32),
+            jax.ShapeDtypeStruct((T, na, ni, nj), f32),
+            jax.ShapeDtypeStruct((T * na, nkl, nb), f32),
         ),
-        in_specs=[anyspace] * 4,
+        in_specs=[anyspace] * 6,
         out_specs=(vmem, vmem),
         scratch_shapes=[
             pltpu.VMEM((2, features, width), bf16),
@@ -326,42 +476,33 @@
             pltpu.VMEM((T, 4 * rows, cols), f32),
             pltpu.VMEM((2, T, PIECES, 4 * rows // PIECES, cols), bf16),
             pltpu.VMEM((2, T, PIECES, 4 * rows // PIECES, cols), bf16),
+            pltpu.VMEM((4, rows, features), bf16),
+            pltpu.VMEM((4 * rows, cols), f32),
+            pltpu.VMEM((T, na, ni, nj), bf16),
+            pltpu.VMEM((na, T, nkl, nb), bf16),
+            pltpu.VMEM((4 * nf, features), bf16),
+            pltpu.VMEM((na * nk, 4 * nf), bf16),
+            pltpu.VMEM((4, 4 * rows, nf), bf16),
+            pltpu.VMEM((4, 4 * rows, nf), bf16),
+            pltpu.VMEM((4 * rows, na * nk), f32),
+            pltpu.VMEM((4, 4 * rows, nf), bf16),
+            pltpu.VMEM((4, 4 * rows, nf), bf16),
+            pltpu.VMEM((4, na, ni, nj), f32),
+            pltpu.VMEM((na, T, nkl, nb), f32),
             dma((4,)), dma((3,)), dma((3, 2)),
             dma((n,)), dma((n,)), dma((n,)), dma((n,)),
             dma((n,)), dma((n,)), dma((n,)), dma((n,)), dma((n,)), dma((n,)),
             dma((2, T, PIECES)), dma((2, T, PIECES)),
+            dma((T,)), dma((T,)), dma((T,)), dma((T,)),
+            dma((3,)), dma((3,)), dma((3,)), dma((3,)),
+            dma((T,)), dma((T,)), dma((T,)), dma((T,)),
         ],
         compiler_params=pltpu.CompilerParams(
             collective_id=0, has_side_effects=True, vmem_limit_bytes=62 * 1024 * 1024
         ),
-        name="teacher",
-    )(tokens, gate_weight, up_weight, down_weight)
-
-
-def fused_body(tokens, gate_weight, up_weight, down_weight, right_factor, left_factor):
-    T = lax.axis_size("tensor")
-    rows = tokens.shape[0] * lax.axis_size("fsdp")
-    right = lax.all_to_all(right_factor, "tensor", split_axis=1, concat_axis=1, tiled=True)
-    left = lax.all_to_all(left_factor, "tensor", split_axis=0, concat_axis=1, tiled=True)
-    spread, target = teacher(tokens, gate_weight, up_weight, down_weight, T)
-    blocks, size = right.shape[0], right.shape[2]
-    block_input = spread.reshape(rows, blocks, size)
-    mixed = jnp.einsum(
-        "nij,ikj->nik", block_input, right, preferred_element_type=jnp.float32
-    ).astype(jnp.bfloat16)
-    routed = lax.all_to_all(mixed, "fsdp", split_axis=2, concat_axis=1, tiled=True)
-    student = jnp.einsum("nij,jki->njk", routed, left, preferred_element_type=jnp.float32)
-    out_grad = (student - target.reshape(student.shape)) * (1.0 / math.sqrt(rows))
-    grad_left = jnp.einsum("njk,nij->jki", out_grad, routed.astype(jnp.float32))
-    mixed_grad = jnp.einsum("njk,jki->nij", out_grad, left.astype(jnp.float32)).astype(
-        jnp.bfloat16
-    )
-    returned = lax.all_to_all(mixed_grad, "fsdp", split_axis=1, concat_axis=2, tiled=True)
-    grad_right = jnp.einsum(
-        "nik,nij->ikj", returned.astype(jnp.float32), block_input.astype(jnp.float32)
-    )
-    grad_right = lax.all_to_all(grad_right, "tensor", split_axis=1, concat_axis=1, tiled=True)
-    grad_left = lax.all_to_all(grad_left, "tensor", split_axis=1, concat_axis=0, tiled=True)
+        name="layer",
+    )(tokens, gate_weight, up_weight, down_weight, right, left_factor)
+    grad_right = jnp.transpose(grad_right.reshape(T * na, ni, nj), (1, 0, 2))
     return (grad_right, grad_left)
 
 

time: 215 us -> 172 us (0.80); the launches traced: 212 us -> 171 us
  starting transfers between devices: 30 us -> 0 us
  Pallas kernels: 139 us -> 166 us
  waiting for transfers between devices: 25.6 us -> 0 us
  local copies, waits for them, and re-layouts: 11.6 us -> 5.02 us
  matrix products: 3.67 us -> 0 us
    all_to_all x6 -> x0, starting transfers between devices: 30 us -> none  [the longest x1 7.04 us: fused_body(): lax.all_to_all(left_factor, 'tensor', split_axis=0, concat_axis=1, tiled=...]
    pallas_call x1, Pallas kernels: 139 us -> 166 us  [fused_body(): pl.pallas_call(functools.partial(layer_kernel, n, T, rows, width, cols),...]
    all_to_all x6 -> x0, waiting for transfers between devices: 25.6 us -> none  [the longest x1 6.67 us: fused_body(): lax.all_to_all(mixed, 'fsdp', split_axis=2, concat_axis=1, tiled=True)]
    dot_general x5 -> x0, matrix products: 3.67 us -> none  [the longest x1 1.79 us: fused_body(): jnp.einsum('nik,nij->ikj', returned.astype(jnp.float32), block_input.asty...]
    unnamed x15 -> x2, local copies, waits for them, and re-layouts: 6.78 us -> 3.28 us
    convert_element_type x2 -> x0, local copies, waits for them, and re-layouts: 2.2 us -> none  [the longest x1 1.11 us: fused_body(): mixed = jnp.einsum('nij,ikj->nik', block_input, right, preferred_element_...]
  transfers between devices with their start and end apart: 6 -> 0, of which waited for: 5 -> 0; matrix products, arithmetic and copies ran while one was open for 6% -> 0% of each run, Pallas kernels for 66% -> 0%
where the time goes in v2:
time: 172 us; the launch traced here: 171 us
  Pallas kernels  166 us (97%)
  local copies, waits for them, and re-layouts  5.02 us (3%)
    pallas_call x1, Pallas kernels, fused_body(): pl.pallas_call(functools.partial(layer_kernel, n, T, rows, width, cols),...  166 us

profile of v2, /device:TPU:2, one launch (start us, length us, event | category | flops | bytes accessed | tf_op | source)
XLA Modules:
  0.0 171.3 jit_solution(15971821713064570016)
XLA Ops:
  0.6 1.6 copy.13
  2.2 165.7 %layer.1 = (f32[4,8,16,128]{3,2,1,0:T(8,128)}, f32[32,16,64]{2,1,0:T(8,128)}) custom-call(bf16[128,8192]{1,0:T(8,128)(2,1)} %tok.1, bf16[2048,3584]{1,0:T(8,128)(2,1)} %gw.1, bf16[2048,3584]{1,0:T(8,128)(2,1)} %uw.1, bf16[3584,2048]{1,0:T(8,128)(2,1)} %dw.1, bf16[32,16,128]{2,1,0:T(8,128)(2,1)} %bitcast.7, bf16[32,16,64]{2,1,0:T(8,128)(2,1)} %left.1), custom_call_target="tpu_custom_call" | custom-call | tf_op jit(solution)/shard_map/layer/pallas_call | solution.py:459
  167.9 1.7 %copy.12 = f32[32,16,128]{2,0,1:T(8,128)} copy(f32[32,16,128]{2,1,0:T(8,128)} %bitcast.9) | data formatting | bytes 524288 | tf_op jit(solution)/shard_map/reshape | solution.py:505
  169.7 1.7 copy.15
